TPU v7x, 32 devices: a whole 2x2x4 slice. The times are simulated.
32 devices in a mesh: row: 4 (over z), col: 8 (over y, x, core).
Axes of the slice: x: 2, y: 2, z: 4, core: 2. Of those that a mesh axis runs over, the one named last changes fastest.
Arguments:
- species: float32 [53, 32, 64, 256], P(None, 'row', 'col'), may hold values from 0.05 to 2
- velocity: float32 [3, 32, 64, 256], P(None, 'row', 'col'), may hold values from -1 to 1
- diffusivity: float32 [53], replicated, may hold values from 0.02 to 0.1
- divergence: float32 [32, 64, 256], P('row', 'col'), may hold values from -6 to 6
- log_rates: float32 [325], replicated, may hold values from -3 to 1
- reactants: int32 [325, 53], replicated, may hold values from 0 to 3, as said below
- products: int32 [325, 53], replicated, may hold values from 0 to 3, as said below
- heat_weights: float32 [53], replicated, may hold values from -0.875 to 0.875
- substeps: int32 [32, 64, 2], P('row', 'col'), may hold values from 1 to 6
Outputs:
- reacted: float32 [53, 32, 64, 256], P(None, 'row', 'col')
- pressure: float32 [32, 64, 256], P('row', 'col')
Inputs may be any that keep to these rules, and one draw needn't show every extreme that they name: `reactants`: each reaction has one or two reactant species. `products`: each reaction has one or two product species.
All inputs are finite; a program needn't handle non-finite values.
Results may differ from a plain program's by a relative error of at most 0.0003.
Values sent between devices are 32-bit elements; how exact they have to be, the bound alone decides.
No kernel may reach another device: no remote copies, remote signals or barrier semaphores. Data moves between devices by JAX's collectives and lax.ppermute only.
A program may use at most 128 MiB of HBM per device.

v0:
```python
import math
import jax
import jax.numpy as jnp
from jax import lax
from jax.sharding import PartitionSpec as P

BLOCK = 128
MAXSUB = 6
time_step = 0.2
screen = 0.004
highest = lax.Precision.HIGHEST
group_blocks = 8


def with_halo(block, sides, width):
    for axis, dim in sides:
        count = lax.axis_size(axis)
        forward = [(i, i + 1) for i in range(count - 1)]
        backward = [(target, source) for source, target in forward]
        low = lax.ppermute(
            lax.slice_in_dim(block, block.shape[dim] - width, None, axis=dim), axis, forward
        )
        high = lax.ppermute(lax.slice_in_dim(block, 0, width, axis=dim), axis, backward)
        block = jnp.concatenate([low, block, high], axis=dim)
    return block


def cosine_table(length):
    wave = jnp.arange(length, dtype=jnp.float32)
    sample = jnp.arange(length, dtype=jnp.float32) + 0.5
    weight = jnp.where(wave == 0, jnp.sqrt(1.0 / length), jnp.sqrt(2.0 / length)).astype(
        jnp.float32
    )
    return weight[:, None] * jnp.cos(jnp.pi * wave[:, None] * sample[None, :] / length)


def mode_values(length):
    wave = jnp.arange(length, dtype=jnp.float32)
    return 2.0 - 2.0 * jnp.cos(jnp.pi * wave / length)


def transport(centre, padded, velocity, diffusivity):
    x_minus = padded[:, :-2, 1:-1, 1:-1]
    x_plus = padded[:, 2:, 1:-1, 1:-1]
    y_minus = padded[:, 1:-1, :-2, 1:-1]
    y_plus = padded[:, 1:-1, 2:, 1:-1]
    z_minus = padded[:, 1:-1, 1:-1, :-2]
    z_plus = padded[:, 1:-1, 1:-1, 2:]
    lateral = x_minus + x_plus + (y_minus + y_plus) + (z_minus + z_plus) - 6.0 * centre
    upwind = jnp.maximum(velocity, 0.0)[:, None]
    downwind = jnp.minimum(velocity, 0.0)[:, None]
    carried = upwind[0] * (centre - x_minus) + downwind[0] * (x_plus - centre)
    carried = carried + upwind[1] * (centre - y_minus) + downwind[1] * (y_plus - centre)
    carried = carried + upwind[2] * (centre - z_minus) + downwind[2] * (z_plus - centre)
    return centre + time_step * (diffusivity[:, None, None, None] * lateral - carried)


def clamp_edges(padded, position, last_index, dimension):
    extent = padded.shape[dimension]
    lower = jnp.where(
        position == 0,
        lax.slice_in_dim(padded, 1, 2, axis=dimension),
        lax.slice_in_dim(padded, 0, 1, axis=dimension),
    )
    upper = jnp.where(
        position == last_index,
        lax.slice_in_dim(padded, extent - 2, extent - 1, axis=dimension),
        lax.slice_in_dim(padded, extent - 1, extent, axis=dimension),
    )
    return jnp.concatenate(
        [lower, lax.slice_in_dim(padded, 1, extent - 1, axis=dimension), upper], axis=dimension
    )


def react_step(conc, step_size, log_rates, react_float, prod_float):
    rates = jnp.exp(
        log_rates[:, None]
        + jnp.dot(react_float, jnp.log(conc), precision=highest, preferred_element_type=jnp.float32)
    )
    gained = jnp.dot(prod_float.T, rates, precision=highest, preferred_element_type=jnp.float32)
    lost = jnp.dot(react_float.T, rates, precision=highest, preferred_element_type=jnp.float32)
    return conc * (conc + step_size * gained) / (conc + step_size * lost)


def kinetics(blocks, counts, log_rates, react_float, prod_float):
    species_count = blocks.shape[0]
    block_count = blocks.shape[1]
    block_cells = blocks.shape[2]
    group_size = math.gcd(group_blocks, block_count)
    ordering = jnp.argsort(-counts, stable=True)
    current = jnp.take(blocks, ordering, axis=1)
    ordered_counts = jnp.take(counts, ordering)
    step_sizes = time_step / ordered_counts.astype(jnp.float32)
    for level in range(MAXSUB):
        active_count = jnp.sum((ordered_counts > level).astype(jnp.int32))
        turn_count = (active_count + group_size - 1) // group_size

        def one_turn(turn_index, holding, level=level):
            start_block = turn_index * group_size
            section = lax.dynamic_slice_in_dim(holding, start_block, group_size, 1)
            still_live = (
                lax.dynamic_slice_in_dim(ordered_counts, start_block, group_size, 0) > level
            )
            sizes_here = lax.dynamic_slice_in_dim(step_sizes, start_block, group_size, 0)
            cell_sizes = jnp.broadcast_to(sizes_here[:, None], (group_size, block_cells)).reshape(
                group_size * block_cells
            )
            flat_section = section.reshape(species_count, group_size * block_cells)
            fresh = react_step(
                flat_section, cell_sizes[None, :], log_rates, react_float, prod_float
            )
            fresh = fresh.reshape(section.shape)
            updated = jnp.where(still_live[None, :, None], fresh, section)
            return lax.dynamic_update_slice_in_dim(holding, updated, start_block, 1)

        current = lax.fori_loop(0, turn_count, one_turn, current)
    return jnp.take(current, jnp.argsort(ordering), axis=1)


def local(
    species,
    velocity,
    diffusivity,
    divergence,
    log_rates,
    reactants,
    products,
    heat_weights,
    substeps,
):
    species_count, cells_x, cells_y, cells_z = species.shape
    rows_count = lax.axis_size("row")
    cols_count = lax.axis_size("col")
    device_count = rows_count * cols_count
    padded = with_halo(species, (("row", 1), ("col", 2)), 1)
    padded = clamp_edges(padded, lax.axis_index("row"), rows_count - 1, 1)
    padded = clamp_edges(padded, lax.axis_index("col"), cols_count - 1, 2)
    padded = jnp.pad(padded, ((0, 0), (0, 0), (0, 0), (1, 1)), mode="edge")
    moved = transport(species, padded, velocity, diffusivity)
    react_float = reactants.astype(jnp.float32)
    prod_float = products.astype(jnp.float32)
    block_count = substeps.shape[0] * substeps.shape[1] * substeps.shape[2]
    blocks = moved.reshape(species_count, block_count, BLOCK)
    counts = substeps.reshape(block_count)
    reacted = kinetics(blocks, counts, log_rates, react_float, prod_float).reshape(
        species_count, cells_x, cells_y, cells_z
    )
    heat = jnp.einsum("s,sxyz->xyz", heat_weights, reacted - moved, precision=highest) / time_step
    source = divergence - heat
    table_z = cosine_table(cells_z)
    forward = jnp.einsum("kz,xyz->kxy", table_z, source, precision=highest).reshape(
        cells_z, cells_x * cells_y
    )
    planes = lax.all_to_all(forward, ("row", "col"), split_axis=0, concat_axis=1, tiled=True)
    depth = cells_z // device_count
    planes = planes.reshape(depth, rows_count, cols_count, cells_x, cells_y)
    table_x = cosine_table(rows_count * cells_x).reshape(rows_count * cells_x, rows_count, cells_x)
    table_y = cosine_table(cols_count * cells_y).reshape(cols_count * cells_y, cols_count, cells_y)
    spectrum = jnp.einsum("ari,zrcij->zacj", table_x, planes, precision=highest)
    spectrum = jnp.einsum("bcj,zacj->zab", table_y, spectrum, precision=highest)
    device_index = lax.axis_index("row") * cols_count + lax.axis_index("col")
    z_values = lax.dynamic_slice_in_dim(mode_values(cells_z), device_index * depth, depth, 0)
    denominator = (
        screen
        + z_values[:, None, None]
        + mode_values(rows_count * cells_x)[None, :, None]
        + mode_values(cols_count * cells_y)[None, None, :]
    )
    spectrum = spectrum / denominator
    spectrum = jnp.einsum("bcj,zab->zacj", table_y, spectrum, precision=highest)
    spectrum = jnp.einsum("ari,zacj->zrcij", table_x, spectrum, precision=highest)
    outgoing = spectrum.reshape(depth, device_count * cells_x * cells_y)
    columns = lax.all_to_all(outgoing, ("row", "col"), split_axis=1, concat_axis=0, tiled=True)
    columns = columns.reshape(cells_z, cells_x, cells_y)
    pressure = jnp.einsum("kz,kxy->xyz", table_z, columns, precision=highest)
    return (reacted, pressure)


def solution(mesh):
    return jax.shard_map(
        local,
        mesh=mesh,
        in_specs=(
            P(None, "row", "col", None),
            P(None, "row", "col", None),
            P(),
            P("row", "col", None),
            P(),
            P(),
            P(),
            P(),
            P("row", "col", None),
        ),
        out_specs=(P(None, "row", "col", None), P("row", "col", None)),
        check_vma=False,
    )
```

profile of v0, /device:TPU:0, one launch (start us, length us, event | category | flops | bytes accessed | tf_op | source)
XLA Modules:
  0.0 622.2 jit_solution(320372246341972101)
XLA Ops:
  1.9 5.0 collective-permute-start
  9.1 2.5 sort.34
  11.7 2.5 sort.35
  22.7 2.2 constant_dynamic-update-slice_fusion.1
  28.7 3.8 collective-permute-done.3
  32.5 1.9 pad_maximum_fusion
  36.0 4.0 pad_maximum_fusion.1
  40.0 4.0 slice.143
  45.5 4.2 pad_maximum_fusion.2
  49.7 8.3 %fusion.110 = (f32[53,10,10,1]{3,2,1,0:T(8,128)}, f32[53,10,10,1]{3,2,1,0:T(8,128)}) fusion(f32[53,10,10,256]{3,2,1,0:T(8,128)} %pad_maximum_fusion.2), kind=kLoop, calls=%fused_computation.221 | loop fusion | bytes 84800 | tf_op jit(solution)/shard_map/jit(_pad)/slice | solution.py:138
  58.0 12.7 %multiply_add_fusion = f32[53,8,8,256]{3,2,1,0:T(8,128)} fusion(f32[53,8,8,256]{3,2,1,0:T(8,128)S(1)} %copy-done.2, f32[53,10,1,256]{3,2,1,0:T(1,128)S(1)} %get-tuple-element.411, f32[53,10,8,256]{3,2,1,0:T(8,128)S(1)} %slice.143, f32[53,10,1,256]{3,2,1,0:T(1,128)S(1)} %get-tuple-element.410, f32[53,10,10,1]{3,2,1,0:T(8,128)} %get-tuple-element.409, ...), kind=kLoop, calls=%fused_computation.116 | loop fusion | flops 32997376 | bytes 18237044 | tf_op jit(solution)/shard_map/add | solution.py:55
  70.7 4.5 reshape.242
  75.2 5.8 copy.42
  81.0 4.7 gather_fusion.1
  85.7 2.4 select_bitcast_fusion.1
  88.0 2.4 copy.45
  90.4 105.9 %while.60 = (s32[]{:T(128)}, f32[53,128,128]{2,1,0:T(8,128)}, s32[]{:T(128)}, s32[128]{0:T(128)S(1)}, f32[128]{0:T(128)S(1)}, /*index=5*/f32[325]{0:T(512)S(1)},...) while((s32[]{:T(128)}, f32[53,128,128]{2,1,0:T(8,128)}, ...), condition=%wide.region_3.5_spmd, body=%wide.region_2.4_spmd.sunk | while | flops 635695104 | bytes 7966159 | solution.py:116
  95.4 1.7 fusion.215
  102.0 1.7 fusion.215
  108.6 1.7 fusion.215
  115.2 1.7 fusion.215
  121.8 1.7 fusion.215
  128.4 1.7 fusion.215
  135.0 1.7 fusion.215
  141.6 1.7 fusion.215
  148.2 1.7 fusion.215
  154.8 1.7 fusion.215
  161.4 1.7 fusion.215
  168.0 1.7 fusion.215
  174.6 1.7 fusion.215
  181.2 1.7 fusion.215
  187.9 1.7 fusion.215
  194.5 1.7 fusion.215
  196.4 66.1 %while.61 = (s32[]{:T(128)}, f32[53,128,128]{2,1,0:T(8,128)}, s32[]{:T(128)}, s32[128]{0:T(128)S(1)}, f32[128]{0:T(128)S(1)}, /*index=5*/f32[325]{0:T(512)S(1)},...) while((s32[]{:T(128)}, f32[53,128,128]{2,1,0:T(8,128)}, ...), condition=%wide.region_6.8_spmd, body=%wide.region_5.7_spmd.sunk | while | flops 635695104 | bytes 7966159 | solution.py:116
  201.3 1.7 fusion.225
  207.9 1.7 fusion.225
  214.5 1.7 fusion.225
  221.1 1.7 fusion.225
  227.7 1.7 fusion.225
  234.3 1.7 fusion.225
  240.9 1.7 fusion.225
  247.6 1.7 fusion.225
  254.2 1.7 fusion.225
  260.8 1.7 fusion.225
  262.5 26.4 %while.62 = (s32[]{:T(128)}, f32[53,128,128]{2,1,0:T(8,128)}, s32[]{:T(128)}, s32[128]{0:T(128)S(1)}, f32[128]{0:T(128)S(1)}, /*index=5*/f32[325]{0:T(512)S(1)},...) while((s32[]{:T(128)}, f32[53,128,128]{2,1,0:T(8,128)}, ...), condition=%wide.region_9.11_spmd, body=%wide.region_8.10_spmd.sunk | while | flops 635695104 | bytes 7966159 | solution.py:116
  267.4 1.7 fusion.235
  274.0 1.7 fusion.235
  280.6 1.7 fusion.235
  287.2 1.7 fusion.235
  288.9 26.4 %while.63 = (s32[]{:T(128)}, f32[53,128,128]{2,1,0:T(8,128)}, s32[]{:T(128)}, s32[128]{0:T(128)S(1)}, f32[128]{0:T(128)S(1)}, /*index=5*/f32[325]{0:T(512)S(1)},...) while((s32[]{:T(128)}, f32[53,128,128]{2,1,0:T(8,128)}, ...), condition=%wide.region_12.14_spmd, body=%wide.region_11.13_spmd.sunk | while | flops 635695104 | bytes 7966159 | solution.py:116
  315.3 20.2 %while.64 = (s32[]{:T(128)}, f32[53,128,128]{2,1,0:T(8,128)}, s32[]{:T(128)}, s32[128]{0:T(128)S(1)}, f32[128]{0:T(128)S(1)}, /*index=5*/f32[325]{0:T(512)S(1)},...) while((s32[]{:T(128)}, f32[53,128,128]{2,1,0:T(8,128)}, ...), condition=%wide.region_15.17_spmd, body=%wide.region_14.16_spmd.sunk | while | flops 635695104 | bytes 7966159 | solution.py:116
  335.6 6.8 %while.65 = (s32[]{:T(128)}, f32[53,128,128]{2,1,0:T(8,128)}, s32[]{:T(128)}, s32[128]{0:T(128)S(1)}, f32[128]{0:T(128)S(1)}, /*index=5*/f32[325]{0:T(512)S(1)},...) while((s32[]{:T(128)}, f32[53,128,128]{2,1,0:T(8,128)}, ...), condition=%wide.region_18.20_spmd, body=%wide.region_17.19_spmd.sunk | while | flops 635695104 | bytes 7966159 | solution.py:116
  342.3 5.8 copy.46
  348.1 4.7 gather_fusion.2
  352.8 2.4 select_bitcast_fusion
  355.1 2.4 copy.47
  357.5 5.1 reshape.244
  362.6 2.7 sub.104
  365.4 4.1 fusion.54
  372.9 221.0 %all-to-all-start = ((f32[32,1,512]{2,1,0:T(1,128)}), f32[32,1,512]{2,1,0:T(1,128)S(1)}, u32[]{:S(2)}, u32[]{:S(2)}) async-start(f32[32,1,512]{2,1,0:T(1,128)} %reshape.290), calls=%async_computation | async-start | bytes 131072 | tf_op jit(solution)/shard_map/all_to_all | solution.py:154
  593.9 7.4 %all-to-all-done = f32[32,1,512]{2,1,0:T(1,128)S(1)} async-done(((f32[32,1,512]{2,1,0:T(1,128)}), f32[32,1,512]{2,1,0:T(1,128)S(1)}, u32[]{:S(2)}, u32[]{:S(2)}) %all-to-all-start) | async-done | bytes 65568 | tf_op jit(solution)/shard_map/all_to_all | solution.py:154
  603.0 1.8 convolution_bitcast_fusion.1
  608.3 9.1 %all_to_all.32 = f32[32,1,512]{2,1,0:T(1,128)S(1)} all-to-all(f32[32,1,512]{2,1,0:T(1,128)S(1)} %reshape.292), channel_id=1, replica_groups=mesh['row'=4,'col'=8] {'row','col'}, dimensions={0} | all-to-all | bytes 131072 | tf_op jit(solution)/shard_map/all_to_all | solution.py:173
  618.6 3.3 fusion.58
  (462 shorter events, 222.3 us)
Async XLA Ops:
  0.6 364.7 %copy-start = (f32[53]{0:T(128)S(1)}, f32[53]{0:T(128)}, u32[]{:S(2)}) copy-start(f32[53]{0:T(128)} %param.30) | copy-start | bytes 640
  1.9 20.8 %collective-permute-start = (f32[53,1,8,256]{3,2,1,0:T(8,128)S(1)}, f32[53,1,8,256]{3,2,1,0:T(8,128)S(1)}, u32[]{:S(2)}, u32[]{:S(2)}) collective-permute-start(f32[53,1,8,256]{3,2,1,0:T(8,128)S(1)} %get-tuple-element.417), channel_id=1, source_target_pairs={{0,8},{8,16},{16,24},{1,9},{9,17},{17,25},{2,10},{10,18},{18,26},{... | collective-permute-start | bytes 1302536 | tf_op jit(solution)/shard_map/ppermute | solution.py:20
  6.8 18.1 %collective-permute-start.1 = (f32[53,1,8,256]{3,2,1,0:T(8,128)S(1)}, f32[53,1,8,256]{3,2,1,0:T(8,128)S(1)}, u32[]{:S(2)}, u32[]{:S(2)}) collective-permute-start(f32[53,1,8,256]{3,2,1,0:T(8,128)S(1)} %get-tuple-element.416), channel_id=1, source_target_pairs={{8,0},{16,8},{24,16},{9,1},{17,9},{25,17},{10,2},{18,10},{26,18},{... | collective-permute-start | bytes 1302536 | tf_op jit(solution)/shard_map/ppermute | solution.py:23
  22.7 5.9 copy-start.4
  25.7 3.0 collective-permute-start.2
  27.2 5.4 collective-permute-start.3
  49.7 8.3 %copy-start.2 = (f32[53,8,8,256]{3,2,1,0:T(8,128)S(1)}, f32[53,8,8,256]{3,2,1,0:T(8,128)}, u32[]{:S(2)}) copy-start(f32[53,8,8,256]{3,2,1,0:T(8,128)} %param.23) | copy-start | bytes 10420228
  49.7 8.3 %copy-start.5 = (f32[53]{0:T(128)S(1)}, f32[53]{0:T(128)}, u32[]{:S(2)}) copy-start(f32[53]{0:T(128)} %param.25) | copy-start | bytes 640
  88.0 2.4 copy-start.3
  357.5 5.1 copy-start.1
  365.3 4.1 copy-start.6
  372.9 228.5 %all-to-all-start = ((f32[32,1,512]{2,1,0:T(1,128)}), f32[32,1,512]{2,1,0:T(1,128)S(1)}, u32[]{:S(2)}, u32[]{:S(2)}) async-start(f32[32,1,512]{2,1,0:T(1,128)} %reshape.290), calls=%async_computation | async-start | bytes 131072 | tf_op jit(solution)/shard_map/all_to_all | solution.py:154
where the time goes:
time: 630 us; the launch traced here: 622 us
  starting transfers between devices  230 us (37%)
  matrix products  149 us (24%)
  other arithmetic  108 us (17%)
  local copies, waits for them, and re-layouts  107 us (17%)
  waiting for transfers between devices  11.3 us (2%)
  blocking collectives  9.1 us (1%)
    all_to_all x1, starting transfers between devices, local(): lax.all_to_all(forward, ('row', 'col'), split_axis=0, concat_axis=1, tile...  221 us
    dynamic_update_slice x38, other arithmetic, one_turn(): return lax.dynamic_update_slice_in_dim(holding, updated, start_block, 1)  64.9 us
    dot_general x38, matrix products, react_step(): jnp.dot(react_float, jnp.log(conc), precision=highest, preferred_element_...  49.1 us
    dot_general x38, matrix products, react_step(): jnp.dot(prod_float.T, rates, precision=highest, preferred_element_type=jn...  43.7 us
    dot_general x38, matrix products, react_step(): jnp.dot(react_float.T, rates, precision=highest, preferred_element_type=j...  42.6 us
    dynamic_slice x38, local copies, waits for them, and re-layouts, one_turn(): section = lax.dynamic_slice_in_dim(holding, start_block, group_size, 1)  36.1 us
    add x1, other arithmetic, transport(): centre + time_step * (diffusivity[:, None, None, None] * lateral - carried)  12.7 us
  transfers between devices with their start and end apart: 5, of which 3 were waited for; matrix products, arithmetic and copies ran while one was open for 2% of the time, Pallas kernels for 0%

commit v1 on v0

--- a/solution.py
+++ b/solution.py
@@ -151,7 +151,15 @@
     forward = jnp.einsum("kz,xyz->kxy", table_z, source, precision=highest).reshape(
         cells_z, cells_x * cells_y
     )
-    planes = lax.all_to_all(forward, ("row", "col"), split_axis=0, concat_axis=1, tiled=True)
+    planes = jnp.concatenate(
+        lax.all_to_all(
+            jnp.stack(jnp.split(forward, lax.axis_size(("row", "col")), axis=0)),
+            ("row", "col"),
+            0,
+            0,
+        ),
+        axis=1,
+    )
     depth = cells_z // device_count
     planes = planes.reshape(depth, rows_count, cols_count, cells_x, cells_y)
     table_x = cosine_table(rows_count * cells_x).reshape(rows_count * cells_x, rows_count, cells_x)

time: 630 us -> 629 us (level)
  transfers between devices with their start and end apart: 5 -> 5, of which waited for: 3 -> 2; matrix products, arithmetic and copies ran while one was open for 2% -> 3% of each run, Pallas kernels for 0% -> 0%
where the time goes in v1:
time: 629 us; the launch traced here: 622 us
  starting transfers between devices  230 us (37%)
  matrix products  149 us (24%)
  other arithmetic  112 us (18%)
  local copies, waits for them, and re-layouts  104 us (17%)
  waiting for transfers between devices  9.93 us (2%)
  blocking collectives  9.1 us (1%)
    all_to_all x1, starting transfers between devices, local(): lax.all_to_all(jnp.stack(jnp.split(forward, lax.axis_size(('row', 'col'))...  221 us
    dynamic_update_slice x38, other arithmetic, one_turn(): return lax.dynamic_update_slice_in_dim(holding, updated, start_block, 1)  64.7 us
    dot_general x38, matrix products, react_step(): jnp.dot(react_float, jnp.log(conc), precision=highest, preferred_element_...  49.2 us
    dot_general x38, matrix products, react_step(): jnp.dot(prod_float.T, rates, precision=highest, preferred_element_type=jn...  43.7 us
    dot_general x38, matrix products, react_step(): jnp.dot(react_float.T, rates, precision=highest, preferred_element_type=j...  42.9 us
    dynamic_slice x38, local copies, waits for them, and re-layouts, one_turn(): section = lax.dynamic_slice_in_dim(holding, start_block, group_size, 1)  36.1 us
    add x1, other arithmetic, transport(): centre + time_step * (diffusivity[:, None, None, None] * lateral - carried)  15.6 us
  transfers between devices with their start and end apart: 5, of which 2 were waited for; matrix products, arithmetic and copies ran while one was open for 3% of the time, Pallas kernels for 0%

profile of v1, /device:TPU:0, one launch (start us, length us, event | category | flops | bytes accessed | tf_op | source)
XLA Modules:
  0.0 621.8 jit_solution(8798487617708987384)
XLA Ops:
  1.9 5.0 collective-permute-start
  9.1 2.5 sort.34
  11.7 2.5 sort.35
  26.7 2.2 constant_dynamic-update-slice_fusion.1
  34.0 2.5 collective-permute-done.3
  36.5 1.7 pad_maximum_fusion
  39.8 1.9 pad_maximum_fusion.1
  44.8 1.8 pad_maximum_fusion.2
  46.6 5.0 fusion.110
  51.6 15.6 %multiply_add_fusion = f32[53,8,8,256]{3,2,1,0:T(8,128)} fusion(f32[53,8,8,256]{3,2,1,0:T(8,128)} %param.23, f32[53,10,1,256]{3,2,1,0:T(1,128)} %copy-done.1, f32[53,10,8,256]{3,2,1,0:T(8,128)S(1)} %slice.175, f32[53,10,1,256]{3,2,1,0:T(1,128)S(1)} %get-tuple-element.410, f32[53,10,10,1]{3,2,1,0:T(8,128)} %get-tuple-element.409, ...), kind=kLoop, calls=%fused_computation.116 | loop fusion | flops 32997376 | bytes 18237044 | tf_op jit(solution)/shard_map/add | solution.py:55
  67.2 4.7 reshape.301
  71.9 5.8 copy.73
  77.7 4.7 gather_fusion.1
  82.5 2.4 select_bitcast_fusion.1
  84.9 2.4 copy.76
  87.3 105.8 %while.60 = (s32[]{:T(128)}, f32[53,128,128]{2,1,0:T(8,128)}, s32[]{:T(128)}, s32[128]{0:T(128)S(1)}, f32[128]{0:T(128)S(1)}, /*index=5*/f32[325]{0:T(512)S(1)},...) while((s32[]{:T(128)}, f32[53,128,128]{2,1,0:T(8,128)}, ...), condition=%wide.region_3.5_spmd, body=%wide.region_2.4_spmd.sunk | while | flops 635695104 | bytes 7966159 | solution.py:116
  92.2 1.7 fusion.215
  98.8 1.7 fusion.215
  105.4 1.7 fusion.215
  112.1 1.7 fusion.215
  118.7 1.7 fusion.215
  125.3 1.7 fusion.215
  131.9 1.7 fusion.215
  138.5 1.7 fusion.215
  145.1 1.7 fusion.215
  151.7 1.7 fusion.215
  158.3 1.7 fusion.215
  165.0 1.7 fusion.215
  171.6 1.7 fusion.215
  178.2 1.7 fusion.215
  184.8 1.7 fusion.215
  191.4 1.7 fusion.215
  193.1 66.1 %while.61 = (s32[]{:T(128)}, f32[53,128,128]{2,1,0:T(8,128)}, s32[]{:T(128)}, s32[128]{0:T(128)S(1)}, f32[128]{0:T(128)S(1)}, /*index=5*/f32[325]{0:T(512)S(1)},...) while((s32[]{:T(128)}, f32[53,128,128]{2,1,0:T(8,128)}, ...), condition=%wide.region_6.8_spmd, body=%wide.region_5.7_spmd.sunk | while | flops 635695104 | bytes 7966159 | solution.py:116
  198.0 1.7 fusion.225
  204.6 1.7 fusion.225
  211.2 1.7 fusion.225
  217.9 1.7 fusion.225
  224.5 1.7 fusion.225
  231.1 1.7 fusion.225
  237.7 1.7 fusion.225
  244.3 1.7 fusion.225
  259.2 26.8 %while.62 = (s32[]{:T(128)}, f32[53,128,128]{2,1,0:T(8,128)}, s32[]{:T(128)}, s32[128]{0:T(128)S(1)}, f32[128]{0:T(128)S(1)}, /*index=5*/f32[325]{0:T(512)S(1)},...) while((s32[]{:T(128)}, f32[53,128,128]{2,1,0:T(8,128)}, ...), condition=%wide.region_9.11_spmd, body=%wide.region_8.10_spmd.sunk | while | flops 635695104 | bytes 7966159 | solution.py:116
  264.1 1.7 fusion.235
  270.7 1.7 fusion.235
  284.0 1.7 fusion.235
  286.1 26.5 %while.63 = (s32[]{:T(128)}, f32[53,128,128]{2,1,0:T(8,128)}, s32[]{:T(128)}, s32[128]{0:T(128)S(1)}, f32[128]{0:T(128)S(1)}, /*index=5*/f32[325]{0:T(512)S(1)},...) while((s32[]{:T(128)}, f32[53,128,128]{2,1,0:T(8,128)}, ...), condition=%wide.region_12.14_spmd, body=%wide.region_11.13_spmd.sunk | while | flops 635695104 | bytes 7966159 | solution.py:116
  291.0 1.7 fusion.245
  297.6 1.7 fusion.245
  310.8 1.7 fusion.245
  312.5 19.8 %while.64 = (s32[]{:T(128)}, f32[53,128,128]{2,1,0:T(8,128)}, s32[]{:T(128)}, s32[128]{0:T(128)S(1)}, f32[128]{0:T(128)S(1)}, /*index=5*/f32[325]{0:T(512)S(1)},...) while((s32[]{:T(128)}, f32[53,128,128]{2,1,0:T(8,128)}, ...), condition=%wide.region_15.17_spmd, body=%wide.region_14.16_spmd.sunk | while | flops 635695104 | bytes 7966159 | solution.py:116
  332.4 6.8 %while.65 = (s32[]{:T(128)}, f32[53,128,128]{2,1,0:T(8,128)}, s32[]{:T(128)}, s32[128]{0:T(128)S(1)}, f32[128]{0:T(128)S(1)}, /*index=5*/f32[325]{0:T(512)S(1)},...) while((s32[]{:T(128)}, f32[53,128,128]{2,1,0:T(8,128)}, ...), condition=%wide.region_18.20_spmd, body=%wide.region_17.19_spmd.sunk | while | flops 635695104 | bytes 7966159 | solution.py:116
  337.3 1.7 fusion.265
  339.1 5.8 copy.77
  345.0 4.7 gather_fusion.2
  349.7 2.4 select_bitcast_fusion
  352.1 2.3 copy.78
  354.4 4.9 reshape.303
  359.4 3.6 sub.104
  363.0 4.1 fusion.54
  372.3 221.2 %all-to-all-start = ((f32[32,1,512]{2,1,0:T(1,128)}), f32[32,1,512]{2,1,0:T(1,128)S(1)}, u32[]{:S(2)}, u32[]{:S(2)}) async-start(f32[32,1,512]{2,1,0:T(1,128)} %reshape.349), calls=%async_computation | async-start | bytes 131072 | tf_op jit(solution)/shard_map/all_to_all | solution.py:155
  593.5 7.4 %all-to-all-done = f32[32,1,512]{2,1,0:T(1,128)S(1)} async-done(((f32[32,1,512]{2,1,0:T(1,128)}), f32[32,1,512]{2,1,0:T(1,128)S(1)}, u32[]{:S(2)}, u32[]{:S(2)}) %all-to-all-start) | async-done | bytes 65568 | tf_op jit(solution)/shard_map/all_to_all | solution.py:155
  602.6 1.8 convolution_bitcast_fusion.1
  607.9 9.1 %all_to_all.21 = f32[32,1,512]{2,1,0:T(1,128)S(1)} all-to-all(f32[32,1,512]{2,1,0:T(1,128)S(1)} %reshape.351), channel_id=1, replica_groups=mesh['row'=4,'col'=8] {'row','col'}, dimensions={0} | all-to-all | bytes 131072 | tf_op jit(solution)/shard_map/all_to_all | solution.py:181
  618.2 3.3 fusion.58
  (550 shorter events, 229.1 us)
Async XLA Ops:
  0.6 362.4 %copy-start = (f32[53]{0:T(128)S(1)}, f32[53]{0:T(128)}, u32[]{:S(2)}) copy-start(f32[53]{0:T(128)} %param.30) | copy-start | bytes 640
  1.9 24.7 %collective-permute-start = (f32[53,1,8,256]{3,2,1,0:T(8,128)S(1)}, f32[53,1,8,256]{3,2,1,0:T(8,128)S(1)}, u32[]{:S(2)}, u32[]{:S(2)}) collective-permute-start(f32[53,1,8,256]{3,2,1,0:T(8,128)S(1)} %get-tuple-element.417), channel_id=1, source_target_pairs={{0,8},{8,16},{16,24},{1,9},{9,17},{17,25},{2,10},{10,18},{18,26},{... | collective-permute-start | bytes 1302536 | tf_op jit(solution)/shard_map/ppermute | solution.py:20
  6.8 22.1 %collective-permute-start.1 = (f32[53,1,8,256]{3,2,1,0:T(8,128)S(1)}, f32[53,1,8,256]{3,2,1,0:T(8,128)S(1)}, u32[]{:S(2)}, u32[]{:S(2)}) collective-permute-start(f32[53,1,8,256]{3,2,1,0:T(8,128)S(1)} %get-tuple-element.416), channel_id=1, source_target_pairs={{8,0},{16,8},{24,16},{9,1},{17,9},{25,17},{10,2},{18,10},{26,18},{... | collective-permute-start | bytes 1302536 | tf_op jit(solution)/shard_map/ppermute | solution.py:23
  14.8 9.3 %copy-start.4 = (s32[1024]{0:T(1024)}, s32[1024]{0:T(1024)S(1)}, u32[]{:S(2)}) copy-start(s32[1024]{0:T(1024)S(1)} %get-tuple-element.462) | copy-start | bytes 12292
  16.6 7.5 %copy-start.10 = (s32[128]{0:T(128)}, s32[128]{0:T(128)S(1)}, u32[]{:S(2)}) copy-start(s32[128]{0:T(128)S(1)} %get-tuple-element.967) | copy-start | bytes 1540
  26.7 6.5 %copy-start.3 = (f32[3,8,8,256]{3,2,1,0:T(8,128)S(1)}, f32[3,8,8,256]{3,2,1,0:T(8,128)}, u32[]{:S(2)}) copy-start(f32[3,8,8,256]{3,2,1,0:T(8,128)} %param.24) | copy-start | bytes 589828
  29.7 4.3 collective-permute-start.2
  31.2 5.4 collective-permute-start.3
  44.0 0.8 copy-start.1
  77.7 4.7 copy-start.12
  84.8 2.4 copy-start.2
  84.9 2.4 copy-start.11
  84.9 2.4 copy-start.15
  345.0 4.7 copy-start.16
  363.0 4.2 copy-start.5
  363.0 4.2 copy-start.6
  363.0 4.2 copy-start.13
  363.0 4.2 copy-start.17
  367.2 235.4 %copy-start.8 = (f32[32]{0:T(128)S(1)}, f32[32]{0:T(128)}, u32[]{:S(2)}) copy-start(f32[32]{0:T(128)} %get-tuple-element.465) | copy-start | bytes 388
  367.2 235.4 %copy-start.9 = (f32[32]{0:T(128)S(1)}, f32[32]{0:T(128)}, u32[]{:S(2)}) copy-start(f32[32]{0:T(128)} %get-tuple-element.466) | copy-start | bytes 388
  368.5 235.9 %copy-start.7 = (f32[8,32]{1,0:T(8,128)S(1)}, f32[8,32]{1,0:T(8,128)}, u32[]{:S(2)}) copy-start(f32[8,32]{1,0:T(8,128)} %broadcast_add_fusion) | copy-start | bytes 3076
  368.6 235.9 %copy-start.14 = (f32[64]{0:T(128)S(1)}, f32[64]{0:T(128)}, u32[]{:S(2)}) copy-start(f32[64]{0:T(128)} %get-tuple-element.467) | copy-start | bytes 772
  368.6 235.9 %copy-start.18 = (f32[64]{0:T(128)S(1)}, f32[64]{0:T(128)}, u32[]{:S(2)}) copy-start(f32[64]{0:T(128)} %get-tuple-element.468) | copy-start | bytes 772
  372.3 228.6 %all-to-all-start = ((f32[32,1,512]{2,1,0:T(1,128)}), f32[32,1,512]{2,1,0:T(1,128)S(1)}, u32[]{:S(2)}, u32[]{:S(2)}) async-start(f32[32,1,512]{2,1,0:T(1,128)} %reshape.349), calls=%async_computation | async-start | bytes 131072 | tf_op jit(solution)/shard_map/all_to_all | solution.py:155
